TPU v7x, 256 devices: a whole 4x4x8 slice. The times are simulated.
256 devices in a mesh: pair: 64 (over x, z, core), virt: 4 (over y).
Axes of the slice: x: 4, y: 4, z: 8, core: 2. Of those that a mesh axis runs over, the one named last changes fastest.
Arguments:
- amplitudes: bfloat16 [65536, 8, 1024], P('pair', 'virt'), may hold values from -6 to 6
- tile_mask: int32 [65536, 8], P('pair', 'virt'), may hold values from 0 to 1
- integrals: bfloat16 [8, 1024, 1024], P('virt', 'pair'), may hold values from -0.0625 to 0.0625
- pair_energy: float32 [65536], P(('pair', 'virt')), may hold values from -2 to -0.5
- virt_energy: float32 [1024], replicated, may hold values from 0.5 to 3
Outputs:
- update: bfloat16 [65536, 1024], P(('pair', 'virt'))
All inputs are finite; a program needn't handle non-finite values.
Results may differ from a plain program's by a relative error of at most 0.011.
Values may be sent and summed in bfloat16 or wider, within the bound.
A program may use at most 64 MiB of HBM per device.

v0:
```python
import jax
import jax.numpy as jnp
from jax import lax
from jax.sharding import PartitionSpec as P


def on_device(amplitudes, tile_mask, integrals, pair_energy, virt_energy):
    masked = amplitudes * tile_mask.astype(jnp.bfloat16)[:, :, None]
    partial_value = jnp.einsum(
        "ptk,tkn->pn",
        masked,
        lax.all_gather(integrals, "pair", axis=1, tiled=True),
        preferred_element_type=jnp.float32,
    )
    ladder = lax.psum_scatter(
        partial_value.astype(jnp.bfloat16), "virt", scatter_dimension=0, tiled=True
    ).astype(jnp.float32)
    denom = virt_energy[None, :] - pair_energy[:, None]
    return (ladder / denom).astype(jnp.bfloat16)


def solution(mesh):
    placed = (
        P("pair", "virt", None),
        P("pair", "virt"),
        P("virt", "pair", None),
        P(("pair", "virt")),
        P(),
    )
    return jax.shard_map(
        on_device, mesh=mesh, in_specs=placed, out_specs=P(("pair", "virt"), None), check_vma=False
    )
```

profile of v0, /device:TPU:1, one launch (start us, length us, event | category | flops | bytes accessed | tf_op | source)
XLA Modules:
  0.0 140.7 jit_solution(15998661899004031293)
XLA Ops:
  6.5 0.0 all-gather.2.cloned.1.call-start
  6.5 0.7 all-gather.2.cloned.1.call-update
  7.3 0.0 reduce-scatter.2.cloned.1.call-start
  7.3 0.7 convert_element_type.12
  8.0 0.2 copy.6
  8.2 8.0 %broadcast_multiply_fusion = bf16[1024,2,1024]{2,1,0:T(2,128)(2,1)} fusion(bf16[1024,2,1024]{2,1,0:T(2,128)(2,1)} %param.5, bf16[1024,2]{1,0:T(8,128)(2,1)S(1)} %copy.6), kind=kLoop, calls=%fused_computation.3 | loop fusion | flops 2097152 | bytes 8392704 | tf_op jit(solution)/shard_map/mul | solution.py:8
  16.2 0.0 copy-start
  16.2 0.0 copy-start.1
  16.2 77.1 %all-gather.2.cloned.1.call-done = bf16[2,1024,1024]{2,1,0:T(8,128)(2,1)} async-done(((bf16[2,16,1024]{2,1,0:T(8,128)(2,1)}), bf16[2,1024,1024]{2,1,0:T(8,128)(2,1)}) %all-gather.2.cloned.1.call-update) | async-done | bytes 4194320 | tf_op jit(solution)/shard_map/all_gather | solution.py:12
  93.3 9.3 %bitcast_convert_fusion = bf16[1024,1024]{1,0:T(8,128)(2,1)} fusion(bf16[2,1024,1024]{2,1,0:T(8,128)(2,1)} %all-gather.2.cloned.1.call-done, bf16[1024,2,1024]{2,1,0:T(2,128)(2,1)} %broadcast_multiply_fusion), kind=kOutput, calls=%fused_computation | convolution fusion | flops 4296015872 | bytes 10485760 | tf_op jit(solution)/shard_map/ptk,tkn->pn/dot_general | solution.py:9
  102.6 0.0 reduce-scatter.2.cloned.1.call-update
  102.7 29.1 %reduce-scatter.2.cloned.1.call-done = bf16[256,1024]{1,0:T(8,128)(2,1)} async-done(((bf16[1024,1024]{1,0:T(8,128)(2,1)}), bf16[256,1024]{1,0:T(8,128)(2,1)}) %reduce-scatter.2.cloned.1.call-update) | async-done | bytes 524304 | tf_op jit(solution)/shard_map/reduce_scatter | solution.py:15
  131.8 0.0 copy-done
  131.8 0.0 copy-done.1
  131.8 2.1 %divide_convert_fusion = bf16[256,1024]{1,0:T(8,128)(2,1)} fusion(bf16[256,1024]{1,0:T(8,128)(2,1)} %reduce-scatter.2.cloned.1.call-done, f32[256]{0:T(256)S(1)} %copy-done.1, f32[1024]{0:T(1024)S(1)} %copy-done), kind=kLoop, calls=%fused_computation.4 | loop fusion | flops 1048576 | bytes 1053696 | tf_op jit(solution)/shard_map/convert_element_type | solution.py:19
Async XLA Ops:
  6.5 86.8 %all-gather.2.cloned.1.call-start = ((), (), s32[]{:S(2)}) async-start(), calls=%async_computation.1 | async-start | bytes 4259840 | tf_op jit(solution)/shard_map/all_gather | solution.py:12
  7.3 124.5 %reduce-scatter.2.cloned.1.call-start = ((), (), s32[]{:S(2)}) async-start(), calls=%async_computation.2 | async-start | bytes 2621440 | tf_op jit(solution)/shard_map/reduce_scatter | solution.py:15
  16.2 115.6 %copy-start = (f32[1024]{0:T(1024)S(1)}, f32[1024]{0:T(1024)}, u32[]{:S(2)}) copy-start(f32[1024]{0:T(1024)} %param.9) | copy-start | bytes 12292
  16.2 115.6 %copy-start.1 = (f32[256]{0:T(256)S(1)}, f32[256]{0:T(256)}, u32[]{:S(2)}) copy-start(f32[256]{0:T(256)} %param.8) | copy-start | bytes 3076
Sparse Core Ops, SparseCore 0:
  10.1 83.1 all-gather.1
  102.8 28.9 reduce-scatter.1
where the time goes:
time: 141 us
  waiting for transfers between devices  107 us (76%)
  between operations  13.4 us (10%)
  other arithmetic  10.8 us (8%)
  matrix products  9.32 us (7%)
    all_gather x1, waiting for transfers between devices, on_device(): lax.all_gather(integrals, 'pair', axis=1, tiled=True)  77.1 us
    reduce_scatter x1, waiting for transfers between devices, on_device(): lax.psum_scatter(partial_value.astype(jnp.bfloat16), 'virt', scatter_dime...  29.1 us
    dot_general x1, matrix products, on_device(): jnp.einsum('ptk,tkn->pn', masked, lax.all_gather(integrals, 'pair', axis=...  9.32 us
    mul x1, other arithmetic, on_device(): masked = amplitudes * tile_mask.astype(jnp.bfloat16)[:, :, None]  8.03 us
  transfers between devices with their start and end apart: 2, of which 2 were waited for; matrix products, arithmetic and copies ran while one was open for 6% of the time, Pallas kernels for 0%

commit v1 on v0

--- a/solution.py
+++ b/solution.py
@@ -9,7 +9,9 @@
     partial_value = jnp.einsum(
         "ptk,tkn->pn",
         masked,
-        lax.all_gather(integrals, "pair", axis=1, tiled=True),
+        jnp.concatenate(
+            lax.all_to_all(jnp.stack([integrals] * lax.axis_size("pair")), "pair", 0, 0), axis=1
+        ),
         preferred_element_type=jnp.float32,
     )
     ladder = lax.psum_scatter(

time: 141 us -> 167 us (1.18)
  starting transfers between devices: 0.04 us -> 13.3 us
  waiting for transfers between devices: 107 us -> 117 us
  local copies, waits for them, and re-layouts: 0.21 us -> 7 us
  matrix products: 9.32 us -> 5.9 us
    all_to_all x0 -> x1, waiting for transfers between devices: none -> 87.6 us  [on_device(): lax.all_to_all(jnp.stack([integrals] * lax.axis_size('pair')), 'pair', 0, 0)]
    all_gather x1 -> x0, waiting for transfers between devices: 77.1 us -> none  [on_device(): lax.all_gather(integrals, 'pair', axis=1, tiled=True)]
    all_to_all x0 -> x1, starting transfers between devices: none -> 13.3 us  [on_device(): lax.all_to_all(jnp.stack([integrals] * lax.axis_size('pair')), 'pair', 0, 0)]
    dot_general x1, matrix products: 9.32 us -> 5.9 us  [on_device(): jnp.einsum('ptk,tkn->pn', masked, jnp.concatenate(lax.all_to_all(jnp.stac...]
    another operation x0 -> x1, local copies, waits for them, and re-layouts: none -> 3.34 us  [on_device(): jnp.stack([integrals] * lax.axis_size('pair'))]
    reshape x0 -> x1, local copies, waits for them, and re-layouts: none -> 2.8 us  [on_device(): jnp.concatenate(lax.all_to_all(jnp.stack([integrals] * lax.axis_size('pai...]
  transfers between devices with their start and end apart: 2 -> 2, of which waited for: 2 -> 2; matrix products, arithmetic and copies ran while one was open for 6% -> 5% of each run, Pallas kernels for 0% -> 0%
where the time goes in v1:
time: 167 us; the launch traced here: 166 us
  waiting for transfers between devices  117 us (70%)
  between operations  13.4 us (8%)
  starting transfers between devices  13.3 us (8%)
  other arithmetic  10.1 us (6%)
  local copies, waits for them, and re-layouts  7 us (4%)
  matrix products  5.9 us (4%)
    all_to_all x1, waiting for transfers between devices, on_device(): lax.all_to_all(jnp.stack([integrals] * lax.axis_size('pair')), 'pair', 0, 0)  87.6 us
    reduce_scatter x1, waiting for transfers between devices, on_device(): lax.psum_scatter(partial_value.astype(jnp.bfloat16), 'virt', scatter_dime...  29 us
    all_to_all x1, starting transfers between devices, on_device(): lax.all_to_all(jnp.stack([integrals] * lax.axis_size('pair')), 'pair', 0, 0)  13.3 us
    mul x1, other arithmetic, on_device(): masked = amplitudes * tile_mask.astype(jnp.bfloat16)[:, :, None]  8.02 us
    dot_general x1, matrix products, on_device(): jnp.einsum('ptk,tkn->pn', masked, jnp.concatenate(lax.all_to_all(jnp.stac...  5.9 us
    another operation x1, local copies, waits for them, and re-layouts, on_device(): jnp.stack([integrals] * lax.axis_size('pair'))  3.34 us
  transfers between devices with their start and end apart: 2, of which 2 were waited for; matrix products, arithmetic and copies ran while one was open for 5% of the time, Pallas kernels for 0%

profile of v1, /device:TPU:1, one launch (start us, length us, event | category | flops | bytes accessed | tf_op | source)
XLA Modules:
  0.0 166.3 jit_solution(2286762615034849401)
XLA Ops:
  6.5 3.3 %stack.2 = bf16[64,2,16,1024]{3,2,1,0:T(8,128)(2,1)} broadcast(bf16[2,16,1024]{2,1,0:T(8,128)(2,1)} %param.7), dimensions={1,2,3} | broadcast | bytes 4259840 | tf_op jit(solution)/shard_map/stack | solution.py:13
  9.9 0.0 copy-start.1
  9.9 13.3 %all-to-all-start = ((bf16[64,2,16,1024]{3,2,1,0:T(8,128)(2,1)}), bf16[64,2,16,1024]{3,2,1,0:T(8,128)(2,1)}, u32[]{:S(2)}, u32[]{:S(2)}) async-start(bf16[64,2,16,1024]{3,2,1,0:T(8,128)(2,1)} %stack.2), calls=%async_computation | async-start | bytes 8388608 | tf_op jit(solution)/shard_map/all_to_all | solution.py:13
  23.2 0.0 reduce-scatter.2.cloned.1.call-start
  23.2 0.0 copy-done.1
  23.3 0.2 copy.8
  23.5 8.0 %broadcast_multiply_fusion = bf16[1024,2,1024]{2,1,0:T(2,128)(2,1)} fusion(bf16[1024,2,1024]{2,1,0:T(2,128)(2,1)} %param.5, bf16[1024,2]{1,0:T(8,128)(2,1)S(1)} %copy.8), kind=kLoop, calls=%fused_computation.3 | loop fusion | flops 2097152 | bytes 8392704 | tf_op jit(solution)/shard_map/mul | solution.py:8
  31.5 87.6 %all-to-all-done = bf16[64,2,16,1024]{3,2,1,0:T(8,128)(2,1)} async-done(((bf16[64,2,16,1024]{3,2,1,0:T(8,128)(2,1)}), bf16[64,2,16,1024]{3,2,1,0:T(8,128)(2,1)}, u32[]{:S(2)}, u32[]{:S(2)}) %all-to-all-start) | async-done | bytes 4194336 | tf_op jit(solution)/shard_map/all_to_all | solution.py:13
  119.0 0.0 copy-start
  119.0 2.8 %copy.9 = bf16[2,64,16,1024]{3,2,1,0:T(8,128)(2,1)S(1)} copy(bf16[2,64,16,1024]{3,2,0,1:T(8,128)(2,1)} %bitcast) | data formatting | bytes 8388608 | tf_op jit(solution)/shard_map/reshape | solution.py:12
  121.8 0.6 copy-done
  122.5 0.0 copy-start.2
  122.5 0.0 copy-start.3
  122.5 5.9 %bitcast_convert_fusion = bf16[1024,1024]{1,0:T(8,128)(2,1)} fusion(bf16[2,1024,1024]{2,1,0:T(8,128)(2,1)S(1)} %bitcast.5, bf16[1024,2,1024]{2,1,0:T(2,128)(2,1)S(1)} %copy-done), kind=kOutput, calls=%fused_computation | convolution fusion | flops 4296015872 | bytes 10485760 | tf_op jit(solution)/shard_map/ptk,tkn->pn/dot_general | solution.py:9
  128.4 0.0 reduce-scatter.2.cloned.1.call-update
  128.4 29.0 %reduce-scatter.2.cloned.1.call-done = bf16[256,1024]{1,0:T(8,128)(2,1)} async-done(((bf16[1024,1024]{1,0:T(8,128)(2,1)}), bf16[256,1024]{1,0:T(8,128)(2,1)}) %reduce-scatter.2.cloned.1.call-update) | async-done | bytes 524304 | tf_op jit(solution)/shard_map/reduce_scatter | solution.py:17
  157.4 0.0 copy-done.2
  157.4 0.0 copy-done.3
  157.4 2.1 %divide_convert_fusion = bf16[256,1024]{1,0:T(8,128)(2,1)} fusion(bf16[256,1024]{1,0:T(8,128)(2,1)} %reduce-scatter.2.cloned.1.call-done, f32[256]{0:T(256)S(1)} %copy-done.3, f32[1024]{0:T(1024)S(1)} %copy-done.2), kind=kLoop, calls=%fused_computation.4 | loop fusion | flops 1048576 | bytes 1053696 | tf_op jit(solution)/shard_map/convert_element_type | solution.py:21
  (1 shorter events, 0.0 us)
Async XLA Ops:
  9.9 13.4 %copy-start.1 = (s32[1024,2]{0,1:T(2,128)S(1)}, s32[1024,2]{0,1:T(2,128)}, u32[]{:S(2)}) copy-start(s32[1024,2]{0,1:T(2,128)} %param.6) | copy-start | bytes 24580
  9.9 109.2 %all-to-all-start = ((bf16[64,2,16,1024]{3,2,1,0:T(8,128)(2,1)}), bf16[64,2,16,1024]{3,2,1,0:T(8,128)(2,1)}, u32[]{:S(2)}, u32[]{:S(2)}) async-start(bf16[64,2,16,1024]{3,2,1,0:T(8,128)(2,1)} %stack.2), calls=%async_computation | async-start | bytes 8388608 | tf_op jit(solution)/shard_map/all_to_all | solution.py:13
  23.2 134.2 %reduce-scatter.2.cloned.1.call-start = ((), (), s32[]{:S(2)}) async-start(), calls=%async_computation.2 | async-start | bytes 2621440 | tf_op jit(solution)/shard_map/reduce_scatter | solution.py:17
  119.0 3.4 %copy-start = (bf16[1024,2,1024]{2,1,0:T(2,128)(2,1)S(1)}, bf16[1024,2,1024]{2,1,0:T(2,128)(2,1)}, u32[]{:S(2)}) copy-start(bf16[1024,2,1024]{2,1,0:T(2,128)(2,1)} %broadcast_multiply_fusion) | copy-start | bytes 12582916
  122.5 34.9 %copy-start.2 = (f32[1024]{0:T(1024)S(1)}, f32[1024]{0:T(1024)}, u32[]{:S(2)}) copy-start(f32[1024]{0:T(1024)} %param.9) | copy-start | bytes 12292
  122.5 34.9 %copy-start.3 = (f32[256]{0:T(256)S(1)}, f32[256]{0:T(256)}, u32[]{:S(2)}) copy-start(f32[256]{0:T(256)} %param.8) | copy-start | bytes 3076
Sparse Core Ops, SparseCore 0:
  128.5 28.8 reduce-scatter.1
